TPU v7x, 256 devices: a whole 4x4x8 slice. The times are simulated.
256 devices in a mesh: req: 4 (over z_hi, core), ctx: 64 (over x, y, z_lo).
Axes of the slice: x: 4, y: 4, z: 8 (z_hi: 2, z_lo: 4; z = z_hi * 4 + z_lo), core: 2. Of those that a mesh axis runs over, the one named last changes fastest.
Arguments:
- query_rows: bfloat16 [4, 7168, 2048], P('req', 'ctx'), may hold values from -120 to 120
- key_rows: bfloat16 [4, 7168, 1024], P('req', 'ctx'), may hold values from -8 to 8
- value_rows: bfloat16 [4, 7168, 1024], P('req', 'ctx'), may hold values from -6 to 6
- image_starts: int32 [4, 14], P('req'), may hold values from 0 to 6912, as said below
- image_counts: int32 [4], P('req'), may hold values from 1 to 14, as said below
Outputs:
- attended: bfloat16 [4, 7168, 2048], P('req', 'ctx')
Inputs may be any that keep to these rules, and one draw needn't show every extreme that they name: `image_starts`: each request's row holds 14 distinct multiples of 256 in ascending order, always starting with 0; in some request the last entry is (27) * 256; only the first image_counts entries of a request are image blocks. `image_counts`: some request has 14 image blocks.
All inputs are finite; a program needn't handle non-finite values.
Results may differ from a plain program's by a relative error of at most 0.0059.
Values may be sent and summed in bfloat16 or wider, within the bound.
A program may use at most 128 MiB of HBM per device.

v0:
```python
import jax
import jax.numpy as jnp
from jax import lax
from jax.sharding import PartitionSpec as P

HEADS = 16
KV_HEADS = 8
HEAD_DIM = 128
IMG = 256
score_scale = 168.0 ** (-0.5)


def image_ids(position, starts, count):
    index = jnp.arange(starts.shape[0], dtype=jnp.int32)
    inside = (
        (starts[None, :] <= position[:, None])
        & (position[:, None] < starts[None, :] + IMG)
        & (index[None, :] < count)
    )
    return jnp.sum(jnp.where(inside, index[None, :] + 1, 0), axis=1) - 1


def shards(query_rows, key_rows, value_rows, image_starts, image_counts):
    my_index = lax.axis_index("ctx")
    row_count = query_rows.shape[1]
    starts = image_starts[0]
    count = image_counts[0]
    local_pos = jnp.arange(row_count, dtype=jnp.int32)
    query_pos = my_index * row_count + local_pos
    query_ids = image_ids(query_pos, starts, count)
    group = HEADS // KV_HEADS
    query_heads = query_rows[0].reshape(row_count, KV_HEADS, group, HEAD_DIM)
    initial = (
        jnp.full((KV_HEADS, group, row_count), -1e30, jnp.float32),
        jnp.zeros((KV_HEADS, group, row_count), jnp.float32),
        jnp.zeros((KV_HEADS, group, row_count, HEAD_DIM), jnp.float32),
    )

    def add_block(state, key_block, value_block, key_pos):
        key_ids = image_ids(key_pos, starts, count)
        visible = (key_pos[None, :] <= query_pos[:, None]) | (
            key_ids[None, :] == query_ids[:, None]
        ) & (query_ids[:, None] >= 0)

        def update(carried):
            running_max, running_total, running_sum = carried
            scores = (
                jnp.einsum(
                    "qkgd,skd->kgqs", query_heads, key_block, preferred_element_type=jnp.float32
                )
                * score_scale
            )
            scores = jnp.where(visible[None, None], scores, -1e30)
            new_max = jnp.maximum(running_max, jnp.max(scores, axis=-1))
            factor = jnp.exp(running_max - new_max)
            weights = jnp.where(visible[None, None], jnp.exp(scores - new_max[..., None]), 0.0)
            new_total = running_total * factor + jnp.sum(weights, axis=-1)
            product = jnp.einsum(
                "kgqs,skd->kgqd",
                weights.astype(jnp.bfloat16),
                value_block,
                preferred_element_type=jnp.float32,
            )
            return (new_max, new_total, running_sum * factor[..., None] + product)

        return lax.cond(jnp.any(visible), update, lambda carried: carried, state)

    start = jnp.int32(0)
    key_piece = lax.all_gather(key_rows, "ctx", axis=1, tiled=True)
    value_piece = lax.all_gather(value_rows, "ctx", axis=1, tiled=True)
    piece_rows = key_piece.shape[1]
    block_rows = max(
        (size for size in range(1, min(piece_rows, 1024) + 1) if piece_rows % size == 0)
    )
    block_total = piece_rows // block_rows
    key_blocks = key_piece[0].reshape(block_total, block_rows, KV_HEADS, HEAD_DIM)
    value_blocks = value_piece[0].reshape(block_total, block_rows, KV_HEADS, HEAD_DIM)

    def scan_step(carried, items):
        key_block, value_block, block_index = items
        key_pos = start + block_index * block_rows + jnp.arange(block_rows, dtype=jnp.int32)
        return (add_block(carried, key_block, value_block, key_pos), None)

    result, unused = lax.scan(
        scan_step, initial, (key_blocks, value_blocks, jnp.arange(block_total, dtype=jnp.int32))
    )
    final_max, final_total, final_sum = result
    output = final_sum / final_total[..., None]
    output = output.transpose(2, 0, 1, 3).reshape(row_count, HEADS * HEAD_DIM).astype(jnp.bfloat16)
    return output[None]


def solution(mesh):
    return jax.shard_map(
        shards,
        mesh=mesh,
        in_specs=(
            P("req", "ctx", None),
            P("req", "ctx", None),
            P("req", "ctx", None),
            P("req", None),
            P("req"),
        ),
        out_specs=P("req", "ctx", None),
        check_vma=False,
    )
```

profile of v0, /device:TPU:126, one launch (start us, length us, event | category | flops | bytes accessed | tf_op | source)
XLA Modules:
  0.0 935.1 jit_solution(16546968612578805428)
XLA Ops:
  11.6 402.7 %all-gather.3.cloned.1.call-done = bf16[1,7168,1024]{2,1,0:T(8,128)(2,1)} async-done(((bf16[1,112,1024]{2,1,0:T(8,128)(2,1)}), bf16[1,7168,1024]{2,1,0:T(8,128)(2,1)}) %all-gather.3.cloned.1.call-update) | async-done | bytes 14680080 | tf_op jit(solution)/shard_map/all_gather | solution.py:69
  414.3 9.1 copy.17
  423.5 6.5 copy.11
  430.0 388.6 %all-gather.5.cloned.1.call-done = bf16[1,7168,1024]{2,1,0:T(8,128)(2,1)} async-done(((bf16[1,112,1024]{2,1,0:T(8,128)(2,1)}), bf16[1,7168,1024]{2,1,0:T(8,128)(2,1)}) %all-gather.5.cloned.1.call-update) | async-done | bytes 14680080 | tf_op jit(solution)/shard_map/all_gather | solution.py:70
  818.6 9.1 copy.18
  827.7 6.4 copy.13
  834.2 92.3 %while.17 = (s32[]{:T(128)}, f32[8,2,112]{2,1,0:T(2,128)S(1)}, f32[8,2,112]{2,1,0:T(2,128)S(1)}, f32[8,2,112,128]{3,2,1,0:T(8,128)S(1)}, s32[7]{0:T(128)S(1)}, /...) while((s32[]{:T(128)}, f32[8,2,112]{2,1,0:T(2,128)S(1)}, ...), condition=%wide.region_8.9_spmd.clone, body=%wide.region_1.8_spmd.clone.sunk | while | flops 964502272 | bytes 29113972 | solution.py:84
  838.0 9.4 %conditional.3 = ((f32[8,2,112]{2,1,0:T(2,128)S(1)}, f32[8,2,112]{2,1,0:T(2,128)S(1)}, f32[8,2,112,128]{3,2,1,0:T(8,128)S(1)})) conditional(s32[]{:T(128)} %convert_element_type.39, (f32[8,2,112]{2,1,0:T(2,128)S(1)}, f32[8,2,112]{2,1,0:T(2,128)S(1)}, f32[8,2,112,128]{3,2,1,0:T(8,128)S(1)}) %tuple.57, (pred[112,1024]{1,0:T(8,128)(4,1)S(1)}, ...), branch_computations={%region_4.4_spmd, %region_5.7_spmd} | conditional | flops 963841536 | bytes 28967968 | solution.py:66
  843.5 3.9 fusion.13
  851.2 9.4 %conditional.3 = ((f32[8,2,112]{2,1,0:T(2,128)S(1)}, f32[8,2,112]{2,1,0:T(2,128)S(1)}, f32[8,2,112,128]{3,2,1,0:T(8,128)S(1)})) conditional(s32[]{:T(128)} %convert_element_type.39, (f32[8,2,112]{2,1,0:T(2,128)S(1)}, f32[8,2,112]{2,1,0:T(2,128)S(1)}, f32[8,2,112,128]{3,2,1,0:T(8,128)S(1)}) %tuple.57, (pred[112,1024]{1,0:T(8,128)(4,1)S(1)}, ...), branch_computations={%region_4.4_spmd, %region_5.7_spmd} | conditional | flops 963841536 | bytes 28967968 | solution.py:66
  851.2 3.0 fusion.2
  856.7 3.9 fusion.13
  864.4 9.4 %conditional.3 = ((f32[8,2,112]{2,1,0:T(2,128)S(1)}, f32[8,2,112]{2,1,0:T(2,128)S(1)}, f32[8,2,112,128]{3,2,1,0:T(8,128)S(1)})) conditional(s32[]{:T(128)} %convert_element_type.39, (f32[8,2,112]{2,1,0:T(2,128)S(1)}, f32[8,2,112]{2,1,0:T(2,128)S(1)}, f32[8,2,112,128]{3,2,1,0:T(8,128)S(1)}) %tuple.57, (pred[112,1024]{1,0:T(8,128)(4,1)S(1)}, ...), branch_computations={%region_4.4_spmd, %region_5.7_spmd} | conditional | flops 963841536 | bytes 28967968 | solution.py:66
  869.8 3.9 fusion.13
  877.6 9.4 %conditional.3 = ((f32[8,2,112]{2,1,0:T(2,128)S(1)}, f32[8,2,112]{2,1,0:T(2,128)S(1)}, f32[8,2,112,128]{3,2,1,0:T(8,128)S(1)})) conditional(s32[]{:T(128)} %convert_element_type.39, (f32[8,2,112]{2,1,0:T(2,128)S(1)}, f32[8,2,112]{2,1,0:T(2,128)S(1)}, f32[8,2,112,128]{3,2,1,0:T(8,128)S(1)}) %tuple.57, (pred[112,1024]{1,0:T(8,128)(4,1)S(1)}, ...), branch_computations={%region_4.4_spmd, %region_5.7_spmd} | conditional | flops 963841536 | bytes 28967968 | solution.py:66
  877.6 3.0 fusion.2
  883.0 3.9 fusion.13
  890.7 9.4 %conditional.3 = ((f32[8,2,112]{2,1,0:T(2,128)S(1)}, f32[8,2,112]{2,1,0:T(2,128)S(1)}, f32[8,2,112,128]{3,2,1,0:T(8,128)S(1)})) conditional(s32[]{:T(128)} %convert_element_type.39, (f32[8,2,112]{2,1,0:T(2,128)S(1)}, f32[8,2,112]{2,1,0:T(2,128)S(1)}, f32[8,2,112,128]{3,2,1,0:T(8,128)S(1)}) %tuple.57, (pred[112,1024]{1,0:T(8,128)(4,1)S(1)}, ...), branch_computations={%region_4.4_spmd, %region_5.7_spmd} | conditional | flops 963841536 | bytes 28967968 | solution.py:66
  896.2 3.9 fusion.13
  903.9 9.4 %conditional.3 = ((f32[8,2,112]{2,1,0:T(2,128)S(1)}, f32[8,2,112]{2,1,0:T(2,128)S(1)}, f32[8,2,112,128]{3,2,1,0:T(8,128)S(1)})) conditional(s32[]{:T(128)} %convert_element_type.39, (f32[8,2,112]{2,1,0:T(2,128)S(1)}, f32[8,2,112]{2,1,0:T(2,128)S(1)}, f32[8,2,112,128]{3,2,1,0:T(8,128)S(1)}) %tuple.57, (pred[112,1024]{1,0:T(8,128)(4,1)S(1)}, ...), branch_computations={%region_4.4_spmd, %region_5.7_spmd} | conditional | flops 963841536 | bytes 28967968 | solution.py:66
  903.9 3.0 fusion.2
  909.4 3.9 fusion.13
  917.1 9.4 %conditional.3 = ((f32[8,2,112]{2,1,0:T(2,128)S(1)}, f32[8,2,112]{2,1,0:T(2,128)S(1)}, f32[8,2,112,128]{3,2,1,0:T(8,128)S(1)})) conditional(s32[]{:T(128)} %convert_element_type.39, (f32[8,2,112]{2,1,0:T(2,128)S(1)}, f32[8,2,112]{2,1,0:T(2,128)S(1)}, f32[8,2,112,128]{3,2,1,0:T(8,128)S(1)}) %tuple.57, (pred[112,1024]{1,0:T(8,128)(4,1)S(1)}, ...), branch_computations={%region_4.4_spmd, %region_5.7_spmd} | conditional | flops 963841536 | bytes 28967968 | solution.py:66
  922.6 3.9 fusion.13
  (116 shorter events, 51.6 us)
Async XLA Ops:
  6.5 407.8 %all-gather.3.cloned.1.call-start = ((), (), s32[]{:S(2)}) async-start(), calls=%async_computation | async-start | bytes 14909440 | tf_op jit(solution)/shard_map/all_gather | solution.py:69
  7.3 811.3 %all-gather.5.cloned.1.call-start = ((), (), s32[]{:S(2)}) async-start(), calls=%async_computation.1 | async-start | bytes 14909440 | tf_op jit(solution)/shard_map/all_gather | solution.py:70
  827.7 6.5 copy-start
Sparse Core Ops, SparseCore 0:
  9.1 405.1 all-gather.2
  416.1 402.4 all-gather.4
where the time goes:
time: 936 us; the launch traced here: 935 us
  waiting for transfers between devices  793 us (85%)
  matrix products  48.3 us (5%)
  local copies, waits for them, and re-layouts  38.8 us (4%)
  other arithmetic  30.4 us (3%)
  between operations  14.2 us (2%)
  loops' own time  10.6 us (1%)
    all_gather x1, waiting for transfers between devices, shards(): key_piece = lax.all_gather(key_rows, 'ctx', axis=1, tiled=True)  403 us
    all_gather x1, waiting for transfers between devices, shards(): value_piece = lax.all_gather(value_rows, 'ctx', axis=1, tiled=True)  389 us
    unnamed x7, local copies, waits for them, and re-layouts  31.3 us
    dot_general x7, matrix products, update(): jnp.einsum('kgqs,skd->kgqd', weights.astype(jnp.bfloat16), value_block, p...  27.2 us
    dot_general x7, matrix products, update(): jnp.einsum('qkgd,skd->kgqs', query_heads, key_block, preferred_element_ty...  21.2 us
  transfers between devices with their start and end apart: 2, of which 2 were waited for; matrix products, arithmetic and copies ran while one was open for 2% of the time, Pallas kernels for 0%

commit v1 on v0

--- a/solution.py
+++ b/solution.py
@@ -66,7 +66,9 @@
         return lax.cond(jnp.any(visible), update, lambda carried: carried, state)
 
     start = jnp.int32(0)
-    key_piece = lax.all_gather(key_rows, "ctx", axis=1, tiled=True)
+    key_piece = jnp.concatenate(
+        lax.all_to_all(jnp.stack([key_rows] * lax.axis_size("ctx")), "ctx", 0, 0), axis=1
+    )
     value_piece = lax.all_gather(value_rows, "ctx", axis=1, tiled=True)
     piece_rows = key_piece.shape[1]
     block_rows = max(

time: 936 us -> 794 us (0.85)
  waiting for transfers between devices: 793 us -> 634 us
  starting transfers between devices: 0.04 us -> 11 us
    all_to_all x0 -> x1, waiting for transfers between devices: none -> 569 us  [shards(): lax.all_to_all(jnp.stack([key_rows] * lax.axis_size('ctx')), 'ctx', 0, 0)]
    all_gather x1 -> x0, waiting for transfers between devices: 403 us -> none  [shards(): key_piece = lax.all_gather(key_rows, 'ctx', axis=1, tiled=True)]
    all_gather x1, waiting for transfers between devices: 389 us -> 63.8 us  [shards(): value_piece = lax.all_gather(value_rows, 'ctx', axis=1, tiled=True)]
    all_to_all x0 -> x1, starting transfers between devices: none -> 10.9 us  [shards(): lax.all_to_all(jnp.stack([key_rows] * lax.axis_size('ctx')), 'ctx', 0, 0)]
    unnamed x7 -> x9, local copies, waits for them, and re-layouts: 31.3 us -> 31.3 us
where the time goes in v1:
time: 794 us; the launch traced here: 791 us
  waiting for transfers between devices  634 us (80%)
  matrix products  48.4 us (6%)
  local copies, waits for them, and re-layouts  45.5 us (6%)
  other arithmetic  28.8 us (4%)
  between operations  14.2 us (2%)
  starting transfers between devices  11 us (1%)
  loops' own time  9.45 us (1%)
    all_to_all x1, waiting for transfers between devices, shards(): lax.all_to_all(jnp.stack([key_rows] * lax.axis_size('ctx')), 'ctx', 0, 0)  569 us
    all_gather x1, waiting for transfers between devices, shards(): value_piece = lax.all_gather(value_rows, 'ctx', axis=1, tiled=True)  63.8 us
    unnamed x9, local copies, waits for them, and re-layouts  31.3 us
    dot_general x7, matrix products, update(): jnp.einsum('kgqs,skd->kgqd', weights.astype(jnp.bfloat16), value_block, p...  27.2 us
    dot_general x7, matrix products, update(): jnp.einsum('qkgd,skd->kgqs', query_heads, key_block, preferred_element_ty...  21.2 us
    reduce_sum x7, other arithmetic, update(): new_total = running_total * factor + jnp.sum(weights, axis=-1)  16.7 us
  transfers between devices with their start and end apart: 2, of which 2 were waited for; matrix products, arithmetic and copies ran while one was open for 2% of the time, Pallas kernels for 0%

profile of v1, /device:TPU:126, one launch (start us, length us, event | category | flops | bytes accessed | tf_op | source)
XLA Modules:
  0.0 791.1 jit_solution(5427171546747754660)
XLA Ops:
  6.5 8.0 %stack.2 = bf16[64,1,112,1024]{3,2,1,0:T(8,128)(2,1)} broadcast(bf16[112,1024]{1,0:T(8,128)(2,1)} %bitcast.68), dimensions={2,3} | broadcast | bytes 14909440 | tf_op jit(solution)/shard_map/stack | solution.py:70
  14.6 10.9 %all-to-all-start = ((bf16[64,1,112,1024]{3,2,1,0:T(8,128)(2,1)}), bf16[64,1,112,1024]{3,2,1,0:T(8,128)(2,1)}, u32[]{:S(2)}, u32[]{:S(2)}) async-start(bf16[64,1,112,1024]{3,2,1,0:T(8,128)(2,1)} %stack.2), calls=%async_computation | async-start | bytes 29360128 | tf_op jit(solution)/shard_map/all_to_all | solution.py:70
  27.5 569.3 %all-to-all-done = bf16[64,1,112,1024]{3,2,1,0:T(8,128)(2,1)} async-done(((bf16[64,1,112,1024]{3,2,1,0:T(8,128)(2,1)}), bf16[64,1,112,1024]{3,2,1,0:T(8,128)(2,1)}, u32[]{:S(2)}, u32[]{:S(2)}) %all-to-all-start) | async-done | bytes 14680096 | tf_op jit(solution)/shard_map/all_to_all | solution.py:70
  596.8 9.1 %copy.21 = bf16[896,8,8,128]{3,2,1,0:T(8,128)(2,1)S(1)} copy(bf16[896,8,8,128]{3,1,2,0:T(8,128)(2,1)} %bitcast.18) | data formatting | bytes 29360128
  606.0 6.5 copy.15
  612.5 63.8 %all-gather.2.cloned.1.call-done = bf16[1,7168,1024]{2,1,0:T(8,128)(2,1)} async-done(((bf16[1,112,1024]{2,1,0:T(8,128)(2,1)}), bf16[1,7168,1024]{2,1,0:T(8,128)(2,1)}) %all-gather.2.cloned.1.call-update) | async-done | bytes 14680080 | tf_op jit(solution)/shard_map/all_gather | solution.py:72
  676.3 9.1 %copy.22 = bf16[896,8,8,128]{3,2,1,0:T(8,128)(2,1)S(1)} copy(bf16[896,8,8,128]{3,1,2,0:T(8,128)(2,1)} %bitcast.62) | data formatting | bytes 29360128
  685.5 6.4 copy.17
  692.0 90.5 %while.17 = (s32[]{:T(128)}, f32[8,2,112]{2,1,0:T(2,128)S(1)}, f32[8,2,112]{2,1,0:T(2,128)S(1)}, f32[8,2,112,128]{3,2,1,0:T(8,128)S(1)}, s32[7]{0:T(128)S(1)}, /...) while((s32[]{:T(128)}, f32[8,2,112]{2,1,0:T(2,128)S(1)}, ...), condition=%wide.region_8.9_spmd.clone, body=%wide.region_1.8_spmd.clone.sunk | while | flops 964502272 | bytes 29113972 | solution.py:86
  695.5 9.4 %conditional.3 = ((f32[8,2,112]{2,1,0:T(2,128)S(1)}, f32[8,2,112]{2,1,0:T(2,128)S(1)}, f32[8,2,112,128]{3,2,1,0:T(8,128)S(1)})) conditional(s32[]{:T(128)} %convert_element_type.39, (f32[8,2,112]{2,1,0:T(2,128)S(1)}, f32[8,2,112]{2,1,0:T(2,128)S(1)}, f32[8,2,112,128]{3,2,1,0:T(8,128)S(1)}) %tuple.58, (pred[112,1024]{1,0:T(8,128)(4,1)S(1)}, ...), branch_computations={%region_4.4_spmd, %region_5.7_spmd} | conditional | flops 963841536 | bytes 28967968 | solution.py:66
  701.0 3.9 fusion.13
  708.4 9.4 %conditional.3 = ((f32[8,2,112]{2,1,0:T(2,128)S(1)}, f32[8,2,112]{2,1,0:T(2,128)S(1)}, f32[8,2,112,128]{3,2,1,0:T(8,128)S(1)})) conditional(s32[]{:T(128)} %convert_element_type.39, (f32[8,2,112]{2,1,0:T(2,128)S(1)}, f32[8,2,112]{2,1,0:T(2,128)S(1)}, f32[8,2,112,128]{3,2,1,0:T(8,128)S(1)}) %tuple.58, (pred[112,1024]{1,0:T(8,128)(4,1)S(1)}, ...), branch_computations={%region_4.4_spmd, %region_5.7_spmd} | conditional | flops 963841536 | bytes 28967968 | solution.py:66
  708.5 3.0 fusion.2
  713.9 3.9 fusion.13
  721.4 9.4 %conditional.3 = ((f32[8,2,112]{2,1,0:T(2,128)S(1)}, f32[8,2,112]{2,1,0:T(2,128)S(1)}, f32[8,2,112,128]{3,2,1,0:T(8,128)S(1)})) conditional(s32[]{:T(128)} %convert_element_type.39, (f32[8,2,112]{2,1,0:T(2,128)S(1)}, f32[8,2,112]{2,1,0:T(2,128)S(1)}, f32[8,2,112,128]{3,2,1,0:T(8,128)S(1)}) %tuple.58, (pred[112,1024]{1,0:T(8,128)(4,1)S(1)}, ...), branch_computations={%region_4.4_spmd, %region_5.7_spmd} | conditional | flops 963841536 | bytes 28967968 | solution.py:66
  726.8 3.9 fusion.13
  734.3 9.4 %conditional.3 = ((f32[8,2,112]{2,1,0:T(2,128)S(1)}, f32[8,2,112]{2,1,0:T(2,128)S(1)}, f32[8,2,112,128]{3,2,1,0:T(8,128)S(1)})) conditional(s32[]{:T(128)} %convert_element_type.39, (f32[8,2,112]{2,1,0:T(2,128)S(1)}, f32[8,2,112]{2,1,0:T(2,128)S(1)}, f32[8,2,112,128]{3,2,1,0:T(8,128)S(1)}) %tuple.58, (pred[112,1024]{1,0:T(8,128)(4,1)S(1)}, ...), branch_computations={%region_4.4_spmd, %region_5.7_spmd} | conditional | flops 963841536 | bytes 28967968 | solution.py:66
  739.8 3.9 fusion.13
  747.2 9.4 %conditional.3 = ((f32[8,2,112]{2,1,0:T(2,128)S(1)}, f32[8,2,112]{2,1,0:T(2,128)S(1)}, f32[8,2,112,128]{3,2,1,0:T(8,128)S(1)})) conditional(s32[]{:T(128)} %convert_element_type.39, (f32[8,2,112]{2,1,0:T(2,128)S(1)}, f32[8,2,112]{2,1,0:T(2,128)S(1)}, f32[8,2,112,128]{3,2,1,0:T(8,128)S(1)}) %tuple.58, (pred[112,1024]{1,0:T(8,128)(4,1)S(1)}, ...), branch_computations={%region_4.4_spmd, %region_5.7_spmd} | conditional | flops 963841536 | bytes 28967968 | solution.py:66
  752.7 3.9 fusion.13
  760.1 9.4 %conditional.3 = ((f32[8,2,112]{2,1,0:T(2,128)S(1)}, f32[8,2,112]{2,1,0:T(2,128)S(1)}, f32[8,2,112,128]{3,2,1,0:T(8,128)S(1)})) conditional(s32[]{:T(128)} %convert_element_type.39, (f32[8,2,112]{2,1,0:T(2,128)S(1)}, f32[8,2,112]{2,1,0:T(2,128)S(1)}, f32[8,2,112,128]{3,2,1,0:T(8,128)S(1)}) %tuple.58, (pred[112,1024]{1,0:T(8,128)(4,1)S(1)}, ...), branch_computations={%region_4.4_spmd, %region_5.7_spmd} | conditional | flops 963841536 | bytes 28967968 | solution.py:66
  765.6 3.9 fusion.13
  773.1 9.4 %conditional.3 = ((f32[8,2,112]{2,1,0:T(2,128)S(1)}, f32[8,2,112]{2,1,0:T(2,128)S(1)}, f32[8,2,112,128]{3,2,1,0:T(8,128)S(1)})) conditional(s32[]{:T(128)} %convert_element_type.39, (f32[8,2,112]{2,1,0:T(2,128)S(1)}, f32[8,2,112]{2,1,0:T(2,128)S(1)}, f32[8,2,112,128]{3,2,1,0:T(8,128)S(1)}) %tuple.58, (pred[112,1024]{1,0:T(8,128)(4,1)S(1)}, ...), branch_computations={%region_4.4_spmd, %region_5.7_spmd} | conditional | flops 963841536 | bytes 28967968 | solution.py:66
  778.5 3.9 fusion.13
  (118 shorter events, 54.0 us)
Async XLA Ops:
  14.6 12.3 %copy-start = (bf16[1,112,2048]{2,1,0:T(8,128)(2,1)S(1)}, bf16[1,112,2048]{2,1,0:T(8,128)(2,1)}, u32[]{:S(2)}) copy-start(bf16[1,112,2048]{2,1,0:T(8,128)(2,1)} %param.9) | copy-start | bytes 1376260
  14.6 12.8 %copy-start.1 = (s32[1,14]{1,0:T(1,128)S(1)}, s32[1,14]{1,0:T(1,128)}, u32[]{:S(2)}) copy-start(s32[1,14]{1,0:T(1,128)} %param.12) | copy-start | bytes 172
  14.6 582.3 %all-to-all-start = ((bf16[64,1,112,1024]{3,2,1,0:T(8,128)(2,1)}), bf16[64,1,112,1024]{3,2,1,0:T(8,128)(2,1)}, u32[]{:S(2)}, u32[]{:S(2)}) async-start(bf16[64,1,112,1024]{3,2,1,0:T(8,128)(2,1)} %stack.2), calls=%async_computation | async-start | bytes 29360128 | tf_op jit(solution)/shard_map/all_to_all | solution.py:70
  25.5 650.8 %all-gather.2.cloned.1.call-start = ((), (), s32[]{:S(2)}) async-start(), calls=%async_computation.1 | async-start | bytes 14909440 | tf_op jit(solution)/shard_map/all_gather | solution.py:72
Sparse Core Ops, SparseCore 0:
  28.1 648.1 all-gather.1
